TPU v7x, 32 devices: a whole 2x2x4 slice. The times are simulated.
32 devices in a mesh: expert: 4 (over y, core), dp: 8 (over z, x).
Axes of the slice: x: 2, y: 2, z: 4, core: 2. Of those that a mesh axis runs over, the one named last changes fastest.
Arguments:
- tokens: bfloat16 [2048, 3584], P(('dp', 'expert')), parts along dimension 0, may hold values from -6 to 6
- expert_ids: int32 [2048, 1], P(('dp', 'expert')), parts along dimension 0, may hold values from 0 to 3; in each aligned block of 64 rows (0 to 63, 64 to 127, ...) at most 18 rows name the same one
- combine: bfloat16 [2048, 1], P(('dp', 'expert')), parts along dimension 0, may hold values from 0.19921875 to 1
- w_gate: bfloat16 [3584, 8192], P(None, 'expert'), may hold values from -0.09375 to 0.09375
- w_up: bfloat16 [3584, 8192], P(None, 'expert'), may hold values from -0.09375 to 0.09375
- w_down: bfloat16 [8192, 3584], P('expert'), may hold values from -0.125 to 0.125
Outputs:
- mixed: bfloat16 [2048, 3584], P(('dp', 'expert')), parts along dimension 0
There are 8 independent parts, one for each index of `dp`. A program takes and returns all parts, laid end to end along the dimension named above; an argument that names none is the same for every part. Nothing has to cross between parts.
Inputs may be any that keep to these rules, and one draw needn't show every extreme that they name: `expert_ids`: each token names one expert. Among the 64 tokens of one device (aligned blocks of rows) no expert is named more than 18 times, a bound that some block reaches.
All inputs are finite; a program needn't handle non-finite values.
Results may differ from a plain program's by a relative error of at most 0.0057.
Values may be sent and summed in bfloat16 or wider, within the bound.
A program may use at most 128 MiB of HBM per device.

v0:
```python
import jax
import jax.numpy as jnp
from jax import lax
from jax.sharding import PartitionSpec as P

EXPERTS = 4
TOP = 1
CAP = 18


def local(tokens, expert_ids, combine, w_gate, w_up, w_down):
    devices = lax.axis_size("expert")
    span_size = devices // EXPERTS
    model_width = tokens.shape[1]
    token_count = tokens.shape[0]
    flat_ids = expert_ids.reshape(-1)
    labels = jnp.arange(EXPERTS, dtype=jnp.int32)
    member = (flat_ids[:, None] == labels[None, :]).astype(jnp.int32)
    rank_table = jnp.cumsum(member, axis=0) - 1
    positions = jnp.sum(member * rank_table, axis=1)
    slot_ids = jnp.arange(CAP, dtype=jnp.int32)
    placed = (member.T[:, None, :] == 1) & (positions[None, None, :] == slot_ids[None, :, None])
    repeated = jnp.repeat(tokens, TOP, axis=0)
    outgoing = jnp.einsum(
        "ecf,fd->ecd", placed.astype(jnp.bfloat16), repeated, preferred_element_type=jnp.float32
    ).astype(jnp.bfloat16)
    outgoing = jnp.repeat(outgoing, span_size, axis=0)
    arrived = lax.all_to_all(outgoing, "expert", split_axis=0, concat_axis=0, tiled=True)
    slot_count = arrived.shape[1]
    row_block = arrived.reshape(-1, model_width)
    gate_values = jnp.dot(row_block, w_gate, preferred_element_type=jnp.float32)
    up_values = jnp.dot(row_block, w_up, preferred_element_type=jnp.float32)
    hidden = (jax.nn.silu(gate_values) * up_values).astype(jnp.bfloat16)
    result = (
        jnp.dot(hidden, w_down, preferred_element_type=jnp.float32)
        .astype(jnp.bfloat16)
        .reshape(devices, slot_count, model_width)
    )
    returned_rows = lax.all_to_all(result, "expert", split_axis=0, concat_axis=0, tiled=True)
    summed = jnp.sum(
        returned_rows.astype(jnp.float32).reshape(EXPERTS, span_size, CAP, model_width), axis=1
    )
    weighted = placed.astype(jnp.float32) * combine.astype(jnp.float32).reshape(-1)[None, None, :]
    entry_rows = jnp.einsum("ecf,ecd->fd", weighted, summed, precision=lax.Precision.HIGHEST)
    mixed_rows = jnp.sum(entry_rows.reshape(token_count, TOP, model_width), axis=1)
    return mixed_rows.astype(jnp.bfloat16)


def solution(mesh):
    placed = (
        P(("dp", "expert"), None),
        P(("dp", "expert"), None),
        P(("dp", "expert"), None),
        P(None, "expert"),
        P(None, "expert"),
        P("expert", None),
    )
    return jax.shard_map(
        local, mesh=mesh, in_specs=placed, out_specs=P(("dp", "expert"), None), check_vma=False
    )
```

profile of v0, /device:TPU:0, one launch (start us, length us, event | category | flops | bytes accessed | tf_op | source)
XLA Modules:
  0.0 56.4 jit_solution(2965514269756863854)
XLA Ops:
  0.0 0.0 copy-start
  0.0 0.8 %fusion.5 = s32[64,4]{1,0:T(8,128)S(1)} fusion(s32[64]{0:T(128)} %bitcast.17), kind=kLoop, calls=%fused_computation.12 | loop fusion | flops 512 | bytes 1280 | tf_op jit(solution)/shard_map/convert_element_type | solution.py:18
  0.8 0.7 %convert_compare_fusion = pred[4,64]{1,0:T(4,128)(4,1)S(1)} fusion(s32[64]{0:T(128)} %bitcast.18), kind=kLoop, calls=%fused_computation.20 | loop fusion | flops 768 | bytes 512 | tf_op jit(solution)/shard_map/eq | solution.py:22
  1.4 0.1 reduce_window_sum.11
  1.5 0.8 %select_reduce_fusion = s32[64]{0:T(128)S(1)} fusion(s32[64,4]{1,0:T(8,128)S(1)} %reduce_window_sum.11, s32[64]{0:T(128)} %bitcast.19), kind=kLoop, calls=%fused_computation.10 | loop fusion | flops 960 | bytes 1536 | tf_op jit(solution)/shard_map/reduce_sum | solution.py:20
  2.4 0.0 copy-done
  2.4 0.3 convolution_convert_fusion
  2.7 14.6 %all_to_all.10 = bf16[4,18,3584]{2,1,0:T(8,128)(2,1)S(1)} all-to-all(bf16[4,18,3584]{2,1,0:T(8,128)(2,1)S(1)} %convolution_convert_fusion), channel_id=1, replica_groups=mesh['expert'=4,'dp'=8] {'expert'}, dimensions={0} | all-to-all | bytes 1032192 | tf_op jit(solution)/shard_map/all_to_all | solution.py:28
  17.4 0.2 reshape.60
  17.5 7.8 %fusion.14 = f32[72,2048]{1,0:T(8,128)S(1)} fusion(bf16[72,3584]{1,0:T(8,128)(2,1)S(1)} %reshape.60, bf16[3584,2048]{1,0:T(8,128)(2,1)} %param.9), kind=kOutput, calls=%fused_computation.25 | convolution fusion | flops 1056964608 | bytes 15785984 | tf_op jit(solution)/shard_map/dot_general | solution.py:31
  25.4 0.0 copy-start.1
  25.4 14.6 %convolution_convert_fusion.1 = bf16[72,3584]{1,0:T(8,128)(2,1)S(1)} fusion(bf16[2048,3584]{1,0:T(8,128)(2,1)} %param.11, bf16[72,3584]{1,0:T(8,128)(2,1)S(1)} %reshape.60, bf16[3584,2048]{1,0:T(8,128)(2,1)} %param.10, f32[72,2048]{1,0:T(8,128)S(1)} %fusion.14), kind=kOutput, calls=%fused_computation.2 | convolution fusion | flops 2115072000 | bytes 30982144 | tf_op jit(solution)/shard_map/dot_general | solution.py:35
  40.0 1.0 %reshape.61 = bf16[4,18,3584]{2,1,0:T(8,128)(2,1)} reshape(bf16[72,3584]{1,0:T(8,128)(2,1)S(1)} %convolution_convert_fusion.1) | data formatting | bytes 1032192 | tf_op jit(solution)/shard_map/reshape | solution.py:37
  41.0 3.5 %all-to-all-start.1 = ((bf16[4,18,3584]{2,1,0:T(8,128)(2,1)}), bf16[4,18,3584]{2,1,0:T(8,128)(2,1)S(1)}, u32[]{:S(2)}, u32[]{:S(2)}) async-start(bf16[4,18,3584]{2,1,0:T(8,128)(2,1)} %reshape.61), calls=%async_computation.1 | async-start | bytes 1376256 | tf_op jit(solution)/shard_map/all_to_all | solution.py:39
  44.5 0.0 copy-done.1
  44.5 10.5 %all-to-all-done.1 = bf16[4,18,3584]{2,1,0:T(8,128)(2,1)S(1)} async-done(((bf16[4,18,3584]{2,1,0:T(8,128)(2,1)}), bf16[4,18,3584]{2,1,0:T(8,128)(2,1)S(1)}, u32[]{:S(2)}, u32[]{:S(2)}) %all-to-all-start.1) | async-done | bytes 516128 | tf_op jit(solution)/shard_map/all_to_all | solution.py:39
  55.0 1.4 %fusion = bf16[64,3584]{1,0:T(8,128)(2,1)} fusion(bf16[4,18,3584]{2,1,0:T(8,128)(2,1)S(1)} %all-to-all-done.1, f32[64]{0:T(128)S(1)} %bitcast_convert_fusion, pred[18,64]{1,0:T(8,128)(4,1)S(1)} %iota_compare_fusion.1, pred[4,64]{1,0:T(4,128)(4,1)S(1)} %convert_compare_fusion), kind=kOutput, calls=%fused_computation.3 | convolution fusion | flops 198419456 | bytes 976512 | tf_op jit(solution)/shard_map/ecf,ecd->fd/dot_general | solution.py:44
  (2 shorter events, 0.0 us)
Async XLA Ops:
  0.0 2.4 %copy-start = (bf16[64,3584]{1,0:T(8,128)(2,1)S(1)}, bf16[64,3584]{1,0:T(8,128)(2,1)}, u32[]{:S(2)}) copy-start(bf16[64,3584]{1,0:T(8,128)(2,1)} %param.6) | copy-start | bytes 1376260
  25.4 19.1 %copy-start.1 = (bf16[64,1]{0,1:T(2,128)(2,1)S(1)}, bf16[64,1]{0,1:T(2,128)(2,1)}, u32[]{:S(2)}) copy-start(bf16[64,1]{0,1:T(2,128)(2,1)} %param.8) | copy-start | bytes 388
  41.0 14.0 %all-to-all-start.1 = ((bf16[4,18,3584]{2,1,0:T(8,128)(2,1)}), bf16[4,18,3584]{2,1,0:T(8,128)(2,1)S(1)}, u32[]{:S(2)}, u32[]{:S(2)}) async-start(bf16[4,18,3584]{2,1,0:T(8,128)(2,1)} %reshape.61), calls=%async_computation.1 | async-start | bytes 1376256 | tf_op jit(solution)/shard_map/all_to_all | solution.py:39
where the time goes:
time: 56.7 us; the launch traced here: 56.4 us
  matrix products  24.1 us (43%)
  blocking collectives  14.6 us (26%)
  waiting for transfers between devices  10.5 us (19%)
  starting transfers between devices  3.48 us (6%)
  other arithmetic  2.38 us (4%)
  local copies, waits for them, and re-layouts  1.19 us (2%)
    all_to_all x1, blocking collectives, local(): lax.all_to_all(outgoing, 'expert', split_axis=0, concat_axis=0, tiled=True)  14.6 us
    dot_general x1, matrix products, local(): jnp.dot(hidden, w_down, preferred_element_type=jnp.float32)  14.6 us
    all_to_all x1, waiting for transfers between devices, local(): lax.all_to_all(result, 'expert', split_axis=0, concat_axis=0, tiled=True)  10.5 us
    dot_general x1, matrix products, local(): gate_values = jnp.dot(row_block, w_gate, preferred_element_type=jnp.float32)  7.85 us
    all_to_all x1, starting transfers between devices, local(): lax.all_to_all(result, 'expert', split_axis=0, concat_axis=0, tiled=True)  3.48 us
    dot_general x1, matrix products, local(): jnp.einsum('ecf,ecd->fd', weighted, summed, precision=lax.Precision.HIGHEST)  1.35 us
  transfers between devices with their start and end apart: 1, of which 1 were waited for; matrix products, arithmetic and copies ran while one was open for 0% of the time, Pallas kernels for 0%

commit v1 on v0

v1 whole, which is shorter than its diff:
```python
import functools

import jax
import jax.numpy as jnp
from jax import lax
from jax.experimental import pallas as pl
from jax.experimental.pallas import tpu as pltpu
from jax.sharding import PartitionSpec as P

EXPERTS = 4
TOP = 1
CAP = 18
MAIN = 16
EXTRA = CAP - MAIN
FOLD = 8
LANES = 128
PIECES = FOLD // EXTRA
CHUNK = PIECES * LANES
BF16, F32, I32 = jnp.bfloat16, jnp.float32, jnp.int32


def iota(shape, axis):
    return lax.broadcasted_iota(I32, shape, axis)


def dot(a, b):
    return jnp.dot(a, b, preferred_element_type=F32)


def kernel(
    n, span, chunks, tokens_hbm, ids_hbm, combine_hbm, gate_hbm, up_hbm, down_hbm, out_hbm,
    tokens, ids, combine, gate, up, down, send_m, send_e, recv_m, recv_e, gate_sum, up_sum,
    hidden, out, back_m, back_e, home_m, home_e,
    small_sem, gate_sem, up_sem, down_sem, out_sem, send_sem, recv_sem, back_sem, home_sem,
):
    me = lax.axis_index("expert")
    count = tokens.shape[0]
    width = gate.shape[2]
    extra_rows = -(-EXTRA * n // MAIN) * MAIN
    chip, core = me // 2, me % 2

    peers = []
    for step in range(1, n // 2):
        for turn in range(2):
            peers.append((chip + step) % (n // 2) * 2 + (core + turn) % 2)
    peers.append(chip * 2 + (core + 1) % 2)

    barrier = pltpu.get_barrier_semaphore()
    for peer in peers:
        pl.semaphore_signal(barrier, inc=1, device_id={"expert": peer})

    first = [
        pltpu.make_async_copy(ids_hbm, ids, small_sem.at[0]),
        pltpu.make_async_copy(tokens_hbm, tokens, small_sem.at[1]),
        pltpu.make_async_copy(combine_hbm, combine, small_sem.at[2]),
    ]
    for copy in first:
        copy.start()

    def gate_copy(k):
        rows = pl.ds(pl.multiple_of(k * CHUNK, CHUNK), CHUNK)
        return pltpu.make_async_copy(gate_hbm.at[rows, :], gate.at[k], gate_sem.at[k])

    def up_copy(k):
        rows = pl.ds(pl.multiple_of(k * CHUNK, CHUNK), CHUNK)
        return pltpu.make_async_copy(up_hbm.at[rows, :], up.at[k], up_sem.at[k])

    def down_copy(k):
        columns = pl.ds(pl.multiple_of(k * CHUNK, CHUNK), CHUNK)
        return pltpu.make_async_copy(down_hbm.at[:, columns], down.at[k], down_sem.at[k])

    def out_copy(k):
        columns = pl.ds(pl.multiple_of(k * CHUNK, CHUNK), CHUNK)
        return pltpu.make_async_copy(out.at[k], out_hbm.at[:, columns], out_sem.at[k])

    def start_in(k, _):
        gate_copy(k).start()
        up_copy(k).start()
        return 0

    def start_down(k, _):
        down_copy(k).start()
        return 0

    lax.fori_loop(0, chunks, start_in, 0)
    lax.fori_loop(0, chunks, start_down, 0)

    first[0].wait()
    own = ids[...]
    member = iota((8, count), 0) == own
    earlier = (iota((count, count), 0) < iota((count, count), 1)).astype(F32).astype(BF16)
    ranks = dot(member.astype(F32).astype(BF16), earlier)
    place = jnp.sum(jnp.where(member, ranks, 0.0), axis=0, keepdims=True).astype(I32)
    low, high = own * span, own * span + span

    def main_mask():
        row = iota((n * MAIN, count), 0)
        block = row // MAIN
        return (block >= low) & (block < high) & (row - block * MAIN == place)

    def extra_mask(piece):
        row = iota((n * FOLD, count), 0)
        block = row // FOLD
        inner = row - block * FOLD - piece * EXTRA
        return (block >= low) & (block < high) & (inner >= 0) & (inner < EXTRA) & (inner + MAIN == place)

    pick_main = jnp.where(main_mask(), 1.0, 0.0).astype(BF16)
    pick_extra = [jnp.where(extra_mask(j), 1.0, 0.0).astype(BF16) for j in range(PIECES)]

    def send_copies(k, peer):
        return (
            pltpu.make_async_remote_copy(
                src_ref=send_m.at[k, peer], dst_ref=recv_m.at[k, me],
                send_sem=send_sem.at[k, peer, 0], recv_sem=recv_sem.at[k, me, 0],
                device_id={"expert": peer},
            ),
            pltpu.make_async_remote_copy(
                src_ref=send_e.at[k, peer], dst_ref=recv_e.at[k, me],
                send_sem=send_sem.at[k, peer, 1], recv_sem=recv_sem.at[k, me, 1],
                device_id={"expert": peer},
            ),
        )

    def arrivals(k, peer):
        return (
            pltpu.make_async_remote_copy(
                src_ref=send_m.at[k, peer], dst_ref=recv_m.at[k, peer],
                send_sem=send_sem.at[k, peer, 0], recv_sem=recv_sem.at[k, peer, 0],
                device_id={"expert": peer},
            ),
            pltpu.make_async_remote_copy(
                src_ref=send_e.at[k, peer], dst_ref=recv_e.at[k, peer],
                send_sem=send_sem.at[k, peer, 1], recv_sem=recv_sem.at[k, peer, 1],
                device_id={"expert": peer},
            ),
        )

    def back_copies(k, peer):
        return (
            pltpu.make_async_remote_copy(
                src_ref=back_m.at[k, peer], dst_ref=home_m.at[k, me],
                send_sem=back_sem.at[k, peer, 0], recv_sem=home_sem.at[k, me, 0],
                device_id={"expert": peer},
            ),
            pltpu.make_async_remote_copy(
                src_ref=back_e.at[k, peer], dst_ref=home_e.at[k, me],
                send_sem=back_sem.at[k, peer, 1], recv_sem=home_sem.at[k, me, 1],
                device_id={"expert": peer},
            ),
        )

    def returns(k, peer):
        return (
            pltpu.make_async_remote_copy(
                src_ref=back_m.at[k, peer], dst_ref=home_m.at[k, peer],
                send_sem=back_sem.at[k, peer, 0], recv_sem=home_sem.at[k, peer, 0],
                device_id={"expert": peer},
            ),
            pltpu.make_async_remote_copy(
                src_ref=back_e.at[k, peer], dst_ref=home_e.at[k, peer],
                send_sem=back_sem.at[k, peer, 1], recv_sem=home_sem.at[k, peer, 1],
                device_id={"expert": peer},
            ),
        )

    first[1].wait()
    pl.semaphore_wait(barrier, n - 1)

    def dispatch(k, _):
        base = pl.multiple_of(k * CHUNK, CHUNK)
        block = tokens[:, pl.ds(base, CHUNK)]
        send_m[k] = dot(pick_main, block).astype(BF16).reshape(n, MAIN, CHUNK)
        folded = sum(
            dot(pick_extra[j], block[:, j * LANES:(j + 1) * LANES]) for j in range(PIECES)
        )
        send_e[k] = folded.reshape(n, FOLD, LANES).astype(BF16)
        for peer in peers:
            for copy in send_copies(k, peer):
                copy.start()
        recv_m[k, me] = send_m[k, me]
        recv_e[k, me] = send_e[k, me]
        return 0

    lax.fori_loop(0, chunks, dispatch, 0)

    first[2].wait()
    weight = combine[...].astype(F32)
    put_main = jnp.transpose(jnp.where(main_mask(), weight, 0.0)).astype(BF16)
    put_extra = [
        jnp.transpose(jnp.where(extra_mask(j), weight, 0.0)).astype(BF16) for j in range(PIECES)
    ]

    def spread(j):
        row, column = iota((extra_rows, n * FOLD), 0), iota((extra_rows, n * FOLD), 1)
        source = row // EXTRA
        wanted = source * FOLD + j * EXTRA + (row - source * EXTRA)
        return jnp.where(column == wanted, 1.0, 0.0).astype(BF16)

    def fold(j):
        row, column = iota((n * FOLD, extra_rows), 0), iota((n * FOLD, extra_rows), 1)
        source = column // EXTRA
        wanted = source * FOLD + j * EXTRA + (column - source * EXTRA)
        return jnp.where(row == wanted, 1.0, 0.0).astype(BF16)

    spreads = [spread(j) for j in range(PIECES)]
    folds = [fold(j) for j in range(PIECES)]

    def gathered(k):
        for peer in peers:
            for copy in arrivals(k, peer):
                copy.wait_recv()
        extras = recv_e[k].astype(F32).reshape(n * FOLD, LANES).astype(BF16)
        tail = jnp.concatenate([dot(s, extras) for s in spreads], axis=1).astype(BF16)
        return jnp.concatenate([recv_m[k].reshape(n * MAIN, CHUNK), tail], axis=0)

    gate_sum[...] = jnp.zeros_like(gate_sum)
    up_sum[...] = jnp.zeros_like(up_sum)

    def project(k, _):
        rows = gathered(k)
        gate_copy(k).wait()
        gate_sum[...] += dot(rows, gate[k])
        up_copy(k).wait()
        up_sum[...] += dot(rows, up[k])
        return 0

    lax.fori_loop(0, chunks - 1, project, 0)
    last = chunks - 1
    rows = gathered(last)
    gate_copy(last).wait()
    up_copy(last).wait()
    tile = min(512, width)
    for at in range(0, width, tile):
        part = slice(at, at + tile)
        g = gate_sum[:, part] + dot(rows, gate[last, :, part])
        u = up_sum[:, part] + dot(rows, up[last, :, part])
        hidden[:, part] = (g / (1.0 + jnp.exp(-g)) * u).astype(BF16)

    def finish(k, _):
        down_copy(k).wait()
        result = dot(hidden[...], down[k])
        back_m[k] = result[:n * MAIN].astype(BF16).reshape(n, MAIN, CHUNK)
        extra = result[n * MAIN:].astype(BF16)
        folded = sum(dot(folds[j], extra[:, j * LANES:(j + 1) * LANES]) for j in range(PIECES))
        back_e[k] = folded.reshape(n, FOLD, LANES).astype(BF16)
        for peer in peers:
            for copy in back_copies(k, peer):
                copy.start()
        home_m[k, me] = back_m[k, me]
        home_e[k, me] = back_e[k, me]
        return 0

    lax.fori_loop(0, chunks, finish, 0)

    def collect(k, _):
        for peer in peers:
            for copy in returns(k, peer):
                copy.wait_recv()
        main = dot(put_main, home_m[k].reshape(n * MAIN, CHUNK))
        extras = home_e[k].astype(F32).reshape(n * FOLD, LANES).astype(BF16)
        tail = jnp.concatenate([dot(p, extras) for p in put_extra], axis=1)
        out[k] = (main + tail).astype(BF16)
        out_copy(k).start()
        return 0

    lax.fori_loop(0, chunks, collect, 0)

    def drain(k, _):
        for peer in peers:
            for copy in send_copies(k, peer) + back_copies(k, peer):
                copy.wait_send()
        out_copy(k).wait()
        return 0

    lax.fori_loop(0, chunks, drain, 0)


def local(tokens, expert_ids, combine, w_gate, w_up, w_down):
    n = lax.axis_size("expert")
    span = n // EXPERTS
    count, model_width = tokens.shape
    width = w_gate.shape[1]
    chunks = model_width // CHUNK
    extra_rows = -(-EXTRA * n // MAIN) * MAIN
    rows = n * MAIN + extra_rows
    dma = pltpu.SemaphoreType.DMA
    anywhere = pl.BlockSpec(memory_space=pl.ANY)
    return pl.pallas_call(
        functools.partial(kernel, n, span, chunks),
        out_shape=jax.ShapeDtypeStruct((count, model_width), BF16),
        in_specs=[anywhere] * 6,
        out_specs=anywhere,
        scratch_shapes=[
            pltpu.VMEM((count, model_width), BF16),
            pltpu.VMEM((1, count), I32),
            pltpu.VMEM((1, count), BF16),
            pltpu.VMEM((chunks, CHUNK, width), BF16),
            pltpu.VMEM((chunks, CHUNK, width), BF16),
            pltpu.VMEM((chunks, width, CHUNK), BF16),
            pltpu.VMEM((chunks, n, MAIN, CHUNK), BF16),
            pltpu.VMEM((chunks, n, FOLD, LANES), BF16),
            pltpu.VMEM((chunks, n, MAIN, CHUNK), BF16),
            pltpu.VMEM((chunks, n, FOLD, LANES), BF16),
            pltpu.VMEM((rows, width), F32),
            pltpu.VMEM((rows, width), F32),
            pltpu.VMEM((rows, width), BF16),
            pltpu.VMEM((chunks, count, CHUNK), BF16),
            pltpu.VMEM((chunks, n, MAIN, CHUNK), BF16),
            pltpu.VMEM((chunks, n, FOLD, LANES), BF16),
            pltpu.VMEM((chunks, n, MAIN, CHUNK), BF16),
            pltpu.VMEM((chunks, n, FOLD, LANES), BF16),
            dma((3,)),
            dma((chunks,)),
            dma((chunks,)),
            dma((chunks,)),
            dma((chunks,)),
            dma((chunks, n, 2)),
            dma((chunks, n, 2)),
            dma((chunks, n, 2)),
            dma((chunks, n, 2)),
        ],
        compiler_params=pltpu.CompilerParams(
            collective_id=0, has_side_effects=True, vmem_limit_bytes=60 * 1024 * 1024
        ),
    )(
        tokens,
        expert_ids.reshape(1, count),
        combine.reshape(1, count),
        w_gate,
        w_up,
        w_down,
    )


def solution(mesh):
    placed = (
        P(("dp", "expert"), None),
        P(("dp", "expert"), None),
        P(("dp", "expert"), None),
        P(None, "expert"),
        P(None, "expert"),
        P("expert", None),
    )
    return jax.shard_map(
        local, mesh=mesh, in_specs=placed, out_specs=P(("dp", "expert"), None), check_vma=False
    )
```

time: 56.7 us -> 26.9 us (0.47)
  Pallas kernels: 0 us -> 24.9 us
  matrix products: 24.1 us -> 0 us
  blocking collectives: 14.6 us -> 0 us
  waiting for transfers between devices: 10.5 us -> 0 us
  starting transfers between devices: 3.48 us -> 0 us
  other arithmetic: 2.38 us -> 0 us
  local copies, waits for them, and re-layouts: 1.19 us -> 1.82 us
    pallas_call x0 -> x1, Pallas kernels: none -> 24.9 us  [local(): pl.pallas_call(functools.partial(kernel, n, span, chunks), out_shape=jax....]
    dot_general x4 -> x0, matrix products: 24.1 us -> none  [the longest x1 14.6 us: local(): jnp.dot(hidden, w_down, preferred_element_type=jnp.float32)]
    all_to_all x1 -> x0, blocking collectives: 14.6 us -> none  [local(): lax.all_to_all(outgoing, 'expert', split_axis=0, concat_axis=0, tiled=True)]
    all_to_all x1 -> x0, waiting for transfers between devices: 10.5 us -> none  [local(): lax.all_to_all(result, 'expert', split_axis=0, concat_axis=0, tiled=True)]
    all_to_all x1 -> x0, starting transfers between devices: 3.48 us -> none  [local(): lax.all_to_all(result, 'expert', split_axis=0, concat_axis=0, tiled=True)]
    unnamed x4 -> x1, local copies, waits for them, and re-layouts: 0.01 us -> 1.82 us
    reshape x2 -> x0, local copies, waits for them, and re-layouts: 1.18 us -> none  [the longest x1 1.02 us: local(): result = jnp.dot(hidden, w_down, preferred_element_type=jnp.float32).asty...]
    reduce_sum x1 -> x0, other arithmetic: 0.83 us -> none  [local(): positions = jnp.sum(member * rank_table, axis=1)]
  transfers between devices with their start and end apart: 1 -> 0, of which waited for: 1 -> 0; matrix products, arithmetic and copies ran while one was open for 0% -> 0% of each run, Pallas kernels for 0% -> 0%
where the time goes in v1:
time: 26.9 us; the launch traced here: 26.8 us
  Pallas kernels  24.9 us (93%)
  local copies, waits for them, and re-layouts  1.82 us (7%)
    pallas_call x1, Pallas kernels, local(): pl.pallas_call(functools.partial(kernel, n, span, chunks), out_shape=jax....  24.9 us
    unnamed x1, local copies, waits for them, and re-layouts  1.82 us

profile of v1, /device:TPU:0, one launch (start us, length us, event | category | flops | bytes accessed | tf_op | source)
XLA Modules:
  0.0 26.8 jit_solution(1884983788156029471)
XLA Ops:
  0.0 24.9 %shard_map.64 = bf16[64,3584]{1,0:T(8,128)(2,1)} custom-call(bf16[64,3584]{1,0:T(8,128)(2,1)} %tokens_hbm.1, s32[1,64]{1,0:T(1,128)} %bitcast.2, bf16[1,64]{1,0:T(2,128)(2,1)} %bitcast.3, bf16[3584,2048]{1,0:T(8,128)(2,1)} %gate_hbm.1, bf16[3584,2048]{1,0:T(8,128)(2,1)} %up_hbm.1, bf16[2048,3584]{1,0:T(8,128)(2,1)} %down_hbm.1), custom_call_target="tpu_custom_call" | custom-call | tf_op jit(solution)/shard_map/pallas_call | solution.py:288
  24.9 1.8 %copy.8 = bf16[64,3584]{1,0:T(8,128)(2,1)} copy(bf16[64,3584]{1,0:T(8,128)(2,1)} %shard_map.64) | data formatting | bytes 917504

commit v2 on v1

v2 whole, which is shorter than its diff:
```python
import functools

import jax
import jax.numpy as jnp
from jax import lax
from jax.experimental import pallas as pl
from jax.experimental.pallas import tpu as pltpu
from jax.sharding import PartitionSpec as P

EXPERTS = 4
TOP = 1
CAP = 18
MAIN = 16
EXTRA = CAP - MAIN
FOLD = 8
LANES = 128
PIECES = FOLD // EXTRA
CHUNK = PIECES * LANES
BF16, F32, I32 = jnp.bfloat16, jnp.float32, jnp.int32


def iota(shape, axis):
    return lax.broadcasted_iota(I32, shape, axis)


def dot(a, b):
    return jnp.dot(a, b, preferred_element_type=F32)


def kernel(
    n, span, chunks, tokens_hbm, ids_hbm, combine_hbm, gate_hbm, up_hbm, down_hbm, out,
    tokens, ids, combine, gate, up, down, send_m, send_e, recv_m, recv_e, tails, gate_sum, up_sum,
    hidden, back_m, back_e, home_m, home_e,
    small_sem, gate_sem, up_sem, down_sem, send_sem, recv_sem, back_sem, home_sem,
):
    me = lax.axis_index("expert")
    count = tokens.shape[0]
    width = gate.shape[2]
    extra_rows = -(-EXTRA * n // MAIN) * MAIN
    chip, core = me // 2, me % 2

    peers = []
    for step in range(1, n // 2):
        for turn in range(2):
            peers.append((chip + step) % (n // 2) * 2 + (core + turn) % 2)
    peers.append(chip * 2 + (core + 1) % 2)

    barrier = pltpu.get_barrier_semaphore()
    for peer in peers:
        pl.semaphore_signal(barrier, inc=1, device_id={"expert": peer})

    first = [
        pltpu.make_async_copy(ids_hbm, ids, small_sem.at[0]),
        pltpu.make_async_copy(tokens_hbm, tokens, small_sem.at[1]),
        pltpu.make_async_copy(combine_hbm, combine, small_sem.at[2]),
    ]
    for copy in first:
        copy.start()

    def gate_copy(k):
        rows = pl.ds(pl.multiple_of(k * CHUNK, CHUNK), CHUNK)
        return pltpu.make_async_copy(gate_hbm.at[rows, :], gate.at[k], gate_sem.at[k])

    def up_copy(k):
        rows = pl.ds(pl.multiple_of(k * CHUNK, CHUNK), CHUNK)
        return pltpu.make_async_copy(up_hbm.at[rows, :], up.at[k], up_sem.at[k])

    def down_copy(k):
        columns = pl.ds(pl.multiple_of(k * CHUNK, CHUNK), CHUNK)
        return pltpu.make_async_copy(down_hbm.at[:, columns], down.at[k], down_sem.at[k])

    def start_in(k, _):
        gate_copy(k).start()
        up_copy(k).start()
        return 0

    def start_down(k, _):
        down_copy(k).start()
        return 0

    lax.fori_loop(0, chunks, start_in, 0)
    lax.fori_loop(0, chunks, start_down, 0)

    first[0].wait()
    own = ids[...]
    member = iota((8, count), 0) == own
    earlier = (iota((count, count), 0) < iota((count, count), 1)).astype(F32).astype(BF16)
    ranks = dot(member.astype(F32).astype(BF16), earlier)
    place = jnp.sum(jnp.where(member, ranks, 0.0), axis=0, keepdims=True).astype(I32)
    low, high = own * span, own * span + span

    def main_mask():
        row = iota((n * MAIN, count), 0)
        block = row // MAIN
        return (block >= low) & (block < high) & (row - block * MAIN == place)

    def extra_mask(piece):
        row = iota((n * FOLD, count), 0)
        block = row // FOLD
        inner = row - block * FOLD - piece * EXTRA
        return (block >= low) & (block < high) & (inner >= 0) & (inner < EXTRA) & (inner + MAIN == place)

    pick_main = jnp.where(main_mask(), 1.0, 0.0).astype(BF16)
    pick_extra = [jnp.where(extra_mask(j), 1.0, 0.0).astype(BF16) for j in range(PIECES)]

    def send_copies(k, peer, which):
        sources, targets = (send_m, recv_m) if which == 0 else (send_e, recv_e)
        return pltpu.make_async_remote_copy(
            src_ref=sources.at[k, peer], dst_ref=targets.at[k, me],
            send_sem=send_sem.at[k, peer, which], recv_sem=recv_sem.at[k, me, which],
            device_id={"expert": peer},
        )

    def arrivals(k, peer, which):
        sources, targets = (send_m, recv_m) if which == 0 else (send_e, recv_e)
        return pltpu.make_async_remote_copy(
            src_ref=sources.at[k, peer], dst_ref=targets.at[k, peer],
            send_sem=send_sem.at[k, peer, which], recv_sem=recv_sem.at[k, peer, which],
            device_id={"expert": peer},
        )

    def back_copies(k, peer, which):
        sources, targets = (back_m, home_m) if which == 0 else (back_e, home_e)
        return pltpu.make_async_remote_copy(
            src_ref=sources.at[k, peer], dst_ref=targets.at[k, me],
            send_sem=back_sem.at[k, peer, which], recv_sem=home_sem.at[k, me, which],
            device_id={"expert": peer},
        )

    def returns(k, peer, which):
        sources, targets = (back_m, home_m) if which == 0 else (back_e, home_e)
        return pltpu.make_async_remote_copy(
            src_ref=sources.at[k, peer], dst_ref=targets.at[k, peer],
            send_sem=back_sem.at[k, peer, which], recv_sem=home_sem.at[k, peer, which],
            device_id={"expert": peer},
        )

    first[1].wait()
    pl.semaphore_wait(barrier, n - 1)

    def columns_of(k):
        return tokens[:, pl.ds(pl.multiple_of(k * CHUNK, CHUNK), CHUNK)]

    def send_extra(k):
        block = columns_of(k)
        folded = sum(
            dot(pick_extra[j], block[:, j * LANES:(j + 1) * LANES]) for j in range(PIECES)
        )
        send_e[k] = folded.reshape(n, FOLD, LANES).astype(BF16)
        for peer in peers:
            send_copies(k, peer, 1).start()
        recv_e[k, me] = send_e[k, me]

    def send_main(k):
        send_m[k] = dot(pick_main, columns_of(k)).astype(BF16).reshape(n, MAIN, CHUNK)
        for peer in peers:
            send_copies(k, peer, 0).start()
        recv_m[k, me] = send_m[k, me]

    def dispatch(k, _):
        send_extra(k + 1)
        send_main(k)
        return 0

    send_extra(0)
    lax.fori_loop(0, chunks - 1, dispatch, 0)
    send_main(chunks - 1)

    first[2].wait()
    weight = combine[...].astype(F32)
    put_main = jnp.transpose(jnp.where(main_mask(), weight, 0.0)).astype(BF16)
    put_extra = [
        jnp.transpose(jnp.where(extra_mask(j), weight, 0.0)).astype(BF16) for j in range(PIECES)
    ]

    def spread(j):
        row, column = iota((extra_rows, n * FOLD), 0), iota((extra_rows, n * FOLD), 1)
        source = row // EXTRA
        wanted = source * FOLD + j * EXTRA + (row - source * EXTRA)
        return jnp.where(column == wanted, 1.0, 0.0).astype(BF16)

    def fold(j):
        row, column = iota((n * FOLD, extra_rows), 0), iota((n * FOLD, extra_rows), 1)
        source = column // EXTRA
        wanted = source * FOLD + j * EXTRA + (column - source * EXTRA)
        return jnp.where(row == wanted, 1.0, 0.0).astype(BF16)

    spreads = [spread(j) for j in range(PIECES)]
    folds = [fold(j) for j in range(PIECES)]

    def unfold(k):
        extras = recv_e[k].astype(F32).reshape(n * FOLD, LANES).astype(BF16)
        tails[k] = jnp.concatenate([dot(s, extras) for s in spreads], axis=1).astype(BF16)

    def gathered(k):
        return jnp.concatenate([recv_m[k].reshape(n * MAIN, CHUNK), tails[k]], axis=0)

    for peer in peers:
        arrivals(0, peer, 1).wait_recv()
    unfold(0)
    gate_sum[...] = jnp.zeros_like(gate_sum)
    up_sum[...] = jnp.zeros_like(up_sum)

    def project(k, _):
        gate_copy(k).wait()
        up_copy(k).wait()
        for peer in peers:
            arrivals(k + 1, peer, 1).wait_recv()
        for peer in peers:
            arrivals(k, peer, 0).wait_recv()
        rows = gathered(k)
        gate_sum[...] += dot(rows, gate[k])
        up_sum[...] += dot(rows, up[k])
        unfold(k + 1)
        return 0

    lax.fori_loop(0, chunks - 1, project, 0)
    last = chunks - 1
    gate_copy(last).wait()
    up_copy(last).wait()
    for peer in peers:
        arrivals(last, peer, 0).wait_recv()
    rows = gathered(last)
    tile = min(512, width)
    for at in range(0, width, tile):
        part = slice(at, at + tile)
        g = gate_sum[:, part] + dot(rows, gate[last, :, part])
        u = up_sum[:, part] + dot(rows, up[last, :, part])
        hidden[:, part] = (g / (1.0 + jnp.exp(-g)) * u).astype(BF16)

    def finish(k, _):
        down_copy(k).wait()
        result = dot(hidden[...], down[k])
        back_m[k] = result[:n * MAIN].astype(BF16).reshape(n, MAIN, CHUNK)
        for peer in peers:
            back_copies(k, peer, 0).start()
        extra = result[n * MAIN:].astype(BF16)
        folded = sum(dot(folds[j], extra[:, j * LANES:(j + 1) * LANES]) for j in range(PIECES))
        back_e[k] = folded.reshape(n, FOLD, LANES).astype(BF16)
        for peer in peers:
            back_copies(k, peer, 1).start()
        home_m[k, me] = back_m[k, me]
        home_e[k, me] = back_e[k, me]
        return 0

    lax.fori_loop(0, chunks, finish, 0)

    def collect(k, _):
        for peer in peers:
            returns(k, peer, 0).wait_recv()
            returns(k, peer, 1).wait_recv()
        main = dot(put_main, home_m[k].reshape(n * MAIN, CHUNK))
        extras = home_e[k].astype(F32).reshape(n * FOLD, LANES).astype(BF16)
        tail = jnp.concatenate([dot(p, extras) for p in put_extra], axis=1)
        out[:, pl.ds(pl.multiple_of(k * CHUNK, CHUNK), CHUNK)] = (main + tail).astype(BF16)
        return 0

    lax.fori_loop(0, chunks, collect, 0)

    def drain(k, _):
        for peer in peers:
            for which in range(2):
                send_copies(k, peer, which).wait_send()
                back_copies(k, peer, which).wait_send()
        return 0

    lax.fori_loop(0, chunks, drain, 0)


def local(tokens, expert_ids, combine, w_gate, w_up, w_down):
    n = lax.axis_size("expert")
    span = n // EXPERTS
    count, model_width = tokens.shape
    width = w_gate.shape[1]
    chunks = model_width // CHUNK
    extra_rows = -(-EXTRA * n // MAIN) * MAIN
    rows = n * MAIN + extra_rows
    dma = pltpu.SemaphoreType.DMA
    anywhere = pl.BlockSpec(memory_space=pltpu.HBM)
    return pl.pallas_call(
        functools.partial(kernel, n, span, chunks),
        out_shape=jax.ShapeDtypeStruct((count, model_width), BF16),
        in_specs=[anywhere] * 6,
        out_specs=pl.BlockSpec(memory_space=pltpu.VMEM),
        scratch_shapes=[
            pltpu.VMEM((count, model_width), BF16),
            pltpu.VMEM((1, count), I32),
            pltpu.VMEM((1, count), BF16),
            pltpu.VMEM((chunks, CHUNK, width), BF16),
            pltpu.VMEM((chunks, CHUNK, width), BF16),
            pltpu.VMEM((chunks, width, CHUNK), BF16),
            pltpu.VMEM((chunks, n, MAIN, CHUNK), BF16),
            pltpu.VMEM((chunks, n, FOLD, LANES), BF16),
            pltpu.VMEM((chunks, n, MAIN, CHUNK), BF16),
            pltpu.VMEM((chunks, n, FOLD, LANES), BF16),
            pltpu.VMEM((chunks, extra_rows, CHUNK), BF16),
            pltpu.VMEM((rows, width), F32),
            pltpu.VMEM((rows, width), F32),
            pltpu.VMEM((rows, width), BF16),
            pltpu.VMEM((chunks, n, MAIN, CHUNK), BF16),
            pltpu.VMEM((chunks, n, FOLD, LANES), BF16),
            pltpu.VMEM((chunks, n, MAIN, CHUNK), BF16),
            pltpu.VMEM((chunks, n, FOLD, LANES), BF16),
            dma((3,)),
            dma((chunks,)),
            dma((chunks,)),
            dma((chunks,)),
            dma((chunks, n, 2)),
            dma((chunks, n, 2)),
            dma((chunks, n, 2)),
            dma((chunks, n, 2)),
        ],
        compiler_params=pltpu.CompilerParams(
            collective_id=0, vmem_limit_bytes=54 * 1024 * 1024
        ),
    )(
        tokens,
        expert_ids.reshape(1, count),
        combine.reshape(1, count),
        w_gate,
        w_up,
        w_down,
    )


def solution(mesh):
    placed = (
        P(("dp", "expert"), None),
        P(("dp", "expert"), None),
        P(("dp", "expert"), None),
        P(None, "expert"),
        P(None, "expert"),
        P("expert", None),
    )
    return jax.shard_map(
        local, mesh=mesh, in_specs=placed, out_specs=P(("dp", "expert"), None), check_vma=False
    )
```

time: 26.9 us -> 26 us (0.967)
  Pallas kernels: 24.9 us -> 24 us
    pallas_call x1, Pallas kernels: 24.9 us -> 24 us  [local(): pl.pallas_call(functools.partial(kernel, n, span, chunks), out_shape=jax....]
where the time goes in v2:
time: 26 us; the launch traced here: 25.9 us
  Pallas kernels  24 us (92%)
  local copies, waits for them, and re-layouts  1.82 us (7%)
    pallas_call x1, Pallas kernels, local(): pl.pallas_call(functools.partial(kernel, n, span, chunks), out_shape=jax....  24 us
    unnamed x1, local copies, waits for them, and re-layouts  1.82 us

profile of v2, /device:TPU:0, one launch (start us, length us, event | category | flops | bytes accessed | tf_op | source)
XLA Modules:
  0.0 25.9 jit_solution(9810921125345890139)
XLA Ops:
  0.0 24.0 %shard_map.64 = bf16[64,3584]{1,0:T(8,128)(2,1)} custom-call(bf16[64,3584]{1,0:T(8,128)(2,1)} %tokens_hbm.1, s32[1,64]{1,0:T(1,128)} %bitcast.2, bf16[1,64]{1,0:T(2,128)(2,1)} %bitcast.3, bf16[3584,2048]{1,0:T(8,128)(2,1)} %gate_hbm.1, bf16[3584,2048]{1,0:T(8,128)(2,1)} %up_hbm.1, bf16[2048,3584]{1,0:T(8,128)(2,1)} %down_hbm.1), custom_call_target="tpu_custom_call" | custom-call | tf_op jit(solution)/shard_map/pallas_call | solution.py:280
  24.1 1.8 %copy.8 = bf16[64,3584]{1,0:T(8,128)(2,1)} copy(bf16[64,3584]{1,0:T(8,128)(2,1)} %shard_map.64) | data formatting | bytes 917504

commit v3 on v2

--- a/solution.py
+++ b/solution.py
@@ -28,10 +28,10 @@
 
 
 def kernel(
-    n, span, chunks, tokens_hbm, ids_hbm, combine_hbm, gate_hbm, up_hbm, down_hbm, out,
-    tokens, ids, combine, gate, up, down, send_m, send_e, recv_m, recv_e, tails, gate_sum, up_sum,
+    n, span, chunks, tokens, ids, combine, gate_hbm, up_hbm, down_hbm, out,
+    gate, up, down, send_m, send_e, recv_m, recv_e, tails, gate_sum, up_sum,
     hidden, back_m, back_e, home_m, home_e,
-    small_sem, gate_sem, up_sem, down_sem, send_sem, recv_sem, back_sem, home_sem,
+    gate_sem, up_sem, down_sem, send_sem, recv_sem, back_sem, home_sem,
 ):
     me = lax.axis_index("expert")
     count = tokens.shape[0]
@@ -49,14 +49,6 @@
     for peer in peers:
         pl.semaphore_signal(barrier, inc=1, device_id={"expert": peer})
 
-    first = [
-        pltpu.make_async_copy(ids_hbm, ids, small_sem.at[0]),
-        pltpu.make_async_copy(tokens_hbm, tokens, small_sem.at[1]),
-        pltpu.make_async_copy(combine_hbm, combine, small_sem.at[2]),
-    ]
-    for copy in first:
-        copy.start()
-
     def gate_copy(k):
         rows = pl.ds(pl.multiple_of(k * CHUNK, CHUNK), CHUNK)
         return pltpu.make_async_copy(gate_hbm.at[rows, :], gate.at[k], gate_sem.at[k])
@@ -81,7 +73,6 @@
     lax.fori_loop(0, chunks, start_in, 0)
     lax.fori_loop(0, chunks, start_down, 0)
 
-    first[0].wait()
     own = ids[...]
     member = iota((8, count), 0) == own
     earlier = (iota((count, count), 0) < iota((count, count), 1)).astype(F32).astype(BF16)
@@ -135,7 +126,6 @@
             device_id={"expert": peer},
         )
 
-    first[1].wait()
     pl.semaphore_wait(barrier, n - 1)
 
     def columns_of(k):
@@ -166,7 +156,6 @@
     lax.fori_loop(0, chunks - 1, dispatch, 0)
     send_main(chunks - 1)
 
-    first[2].wait()
     weight = combine[...].astype(F32)
     put_main = jnp.transpose(jnp.where(main_mask(), weight, 0.0)).astype(BF16)
     put_extra = [
@@ -276,16 +265,13 @@
     extra_rows = -(-EXTRA * n // MAIN) * MAIN
     rows = n * MAIN + extra_rows
     dma = pltpu.SemaphoreType.DMA
-    anywhere = pl.BlockSpec(memory_space=pltpu.HBM)
+    anywhere = pl.BlockSpec(memory_space=pl.ANY)
     return pl.pallas_call(
         functools.partial(kernel, n, span, chunks),
         out_shape=jax.ShapeDtypeStruct((count, model_width), BF16),
-        in_specs=[anywhere] * 6,
+        in_specs=[pl.BlockSpec(memory_space=pltpu.VMEM)] * 3 + [anywhere] * 3,
         out_specs=pl.BlockSpec(memory_space=pltpu.VMEM),
         scratch_shapes=[
-            pltpu.VMEM((count, model_width), BF16),
-            pltpu.VMEM((1, count), I32),
-            pltpu.VMEM((1, count), BF16),
             pltpu.VMEM((chunks, CHUNK, width), BF16),
             pltpu.VMEM((chunks, CHUNK, width), BF16),
             pltpu.VMEM((chunks, width, CHUNK), BF16),
@@ -301,7 +287,6 @@
             pltpu.VMEM((chunks, n, FOLD, LANES), BF16),
             pltpu.VMEM((chunks, n, MAIN, CHUNK), BF16),
             pltpu.VMEM((chunks, n, FOLD, LANES), BF16),
-            dma((3,)),
             dma((chunks,)),
             dma((chunks,)),
             dma((chunks,)),

time: 26 us -> 27.1 us (1.042)
  Pallas kernels: 24 us -> 25.1 us
    pallas_call x1, Pallas kernels: 24 us -> 25.1 us  [local(): pl.pallas_call(functools.partial(kernel, n, span, chunks), out_shape=jax....]
where the time goes in v3:
time: 27.1 us; the launch traced here: 26.9 us
  Pallas kernels  25.1 us (93%)
  local copies, waits for them, and re-layouts  1.82 us (7%)
    pallas_call x1, Pallas kernels, local(): pl.pallas_call(functools.partial(kernel, n, span, chunks), out_shape=jax....  25.1 us
    unnamed x1, local copies, waits for them, and re-layouts  1.82 us

profile of v3, /device:TPU:0, one launch (start us, length us, event | category | flops | bytes accessed | tf_op | source)
XLA Modules:
  0.0 26.9 jit_solution(5614745230953491320)
XLA Ops:
  0.0 25.1 %shard_map.64 = bf16[64,3584]{1,0:T(8,128)(2,1)} custom-call(bf16[64,3584]{1,0:T(8,128)(2,1)} %tokens.1, s32[1,64]{1,0:T(1,128)} %bitcast.2, bf16[1,64]{1,0:T(2,128)(2,1)} %bitcast.3, bf16[3584,2048]{1,0:T(8,128)(2,1)} %gate_hbm.1, bf16[3584,2048]{1,0:T(8,128)(2,1)} %up_hbm.1, bf16[2048,3584]{1,0:T(8,128)(2,1)} %down_hbm.1), custom_call_target="tpu_custom_call" | custom-call | tf_op jit(solution)/shard_map/pallas_call | solution.py:269
  25.1 1.8 %copy.8 = bf16[64,3584]{1,0:T(8,128)(2,1)} copy(bf16[64,3584]{1,0:T(8,128)(2,1)} %shard_map.64) | data formatting | bytes 917504

commit v4 on v2

--- a/solution.py
+++ b/solution.py
@@ -74,12 +74,7 @@
         up_copy(k).start()
         return 0
 
-    def start_down(k, _):
-        down_copy(k).start()
-        return 0
-
     lax.fori_loop(0, chunks, start_in, 0)
-    lax.fori_loop(0, chunks, start_down, 0)
 
     first[0].wait()
     own = ids[...]
@@ -204,6 +199,7 @@
     def project(k, _):
         gate_copy(k).wait()
         up_copy(k).wait()
+        down_copy(k).start()
         for peer in peers:
             arrivals(k + 1, peer, 1).wait_recv()
         for peer in peers:
@@ -218,6 +214,7 @@
     last = chunks - 1
     gate_copy(last).wait()
     up_copy(last).wait()
+    down_copy(last).start()
     for peer in peers:
         arrivals(last, peer, 0).wait_recv()
     rows = gathered(last)

time: 26 us -> 26 us (level)
  no operation moved by 1% of the time
where the time goes in v4:
time: 26 us; the launch traced here: 25.9 us
  Pallas kernels  24 us (92%)
  local copies, waits for them, and re-layouts  1.82 us (7%)
    pallas_call x1, Pallas kernels, local(): pl.pallas_call(functools.partial(kernel, n, span, chunks), out_shape=jax....  24 us
    unnamed x1, local copies, waits for them, and re-layouts  1.82 us

profile of v4, /device:TPU:0, one launch (start us, length us, event | category | flops | bytes accessed | tf_op | source)
XLA Modules:
  0.0 25.9 jit_solution(2866752839668303308)
XLA Ops:
  0.0 24.0 %shard_map.64 = bf16[64,3584]{1,0:T(8,128)(2,1)} custom-call(bf16[64,3584]{1,0:T(8,128)(2,1)} %tokens_hbm.1, s32[1,64]{1,0:T(1,128)} %bitcast.2, bf16[1,64]{1,0:T(2,128)(2,1)} %bitcast.3, bf16[3584,2048]{1,0:T(8,128)(2,1)} %gate_hbm.1, bf16[3584,2048]{1,0:T(8,128)(2,1)} %up_hbm.1, bf16[2048,3584]{1,0:T(8,128)(2,1)} %down_hbm.1), custom_call_target="tpu_custom_call" | custom-call | tf_op jit(solution)/shard_map/pallas_call | solution.py:277
  24.1 1.8 %copy.8 = bf16[64,3584]{1,0:T(8,128)(2,1)} copy(bf16[64,3584]{1,0:T(8,128)(2,1)} %shard_map.64) | data formatting | bytes 917504
